TPU v7x, 512 devices: a whole 4x4x16 slice. The times are simulated.
512 devices in a mesh: rep: 8 (over y, core), exp: 64 (over x, z).
Axes of the slice: x: 4, y: 4, z: 16, core: 2. Of those that a mesh axis runs over, the one named last changes fastest.
Arguments:
- payload: bfloat16 [16384, 2048], P(('rep', 'exp')), may hold values from -6 to 6
- block_scales: bfloat16 [16384, 16], P(('rep', 'exp')), may hold values from 0.29882812 to 3
- cotangent: bfloat16 [16384, 2048], P(('rep', 'exp')), may hold values from -12 to 12
- expert_ids: int32 [16384, 8], P(('rep', 'exp')), may hold values from 0 to 63, all different within a row; in each aligned block of 32 rows (0 to 31, 32 to 63, ...) at most 5 rows name the same one
- route_counts: int32 [16384, 8], P(('rep', 'exp')), may hold values from 1 to 15
- gate_up: bfloat16 [64, 2, 2048, 384], P('exp', None, 'rep'), may hold values from -0.125 to 0.125
- down_weight: bfloat16 [64, 384, 2048], P('exp', None, 'rep'), may hold values from -0.3125 to 0.3125
- first_moment: float32 [64, 2, 2048, 384], P('exp', None, 'rep'), may hold values from -12 to 12
- second_moment: float32 [64, 2, 2048, 384], P('exp', None, 'rep'), may hold values from 10 to 300
Outputs:
- d_activation: bfloat16 [16384, 2048], P(('rep', 'exp'))
- new_first: float32 [64, 2, 2048, 384], P('exp', None, 'rep')
- new_second: float32 [64, 2, 2048, 384], P('exp', None, 'rep')
- weight_step: bfloat16 [64, 2, 2048, 384], P('exp', None, 'rep')
Inputs may be any that keep to these rules, and one draw needn't show every extreme that they name: `expert_ids`: in the rows of one device (aligned blocks of 32 tokens) no expert is named more than 5 times, a bound that some block reaches; each token names 8 different experts.
All inputs are finite; a program needn't handle non-finite values.
Results may differ from a plain program's by a relative error of at most 0.02.
Values may be sent and summed in bfloat16 or wider, within the bound.
A program may use at most 64 MiB of HBM per device.

v0:
```python
import jax
import jax.numpy as jnp
import numpy as np
from jax import lax
from jax.sharding import PartitionSpec as P

X_SIZE = 4
Z_SIZE = 16
CAPACITY = 5
Z_GROUPS = [[x * Z_SIZE + z for z in range(Z_SIZE)] for x in range(X_SIZE)]
X_GROUPS = [[x * Z_SIZE + z for x in range(X_SIZE)] for z in range(Z_SIZE)]


def silu_parts(gate_pre):
    sigmoid_val = jax.nn.sigmoid(gate_pre)
    return (gate_pre * sigmoid_val, sigmoid_val * (1.0 + gate_pre * (1.0 - sigmoid_val)))


def dequantize(values, scales):
    array_shape = values.shape
    blocked = values.astype(jnp.float32).reshape(
        array_shape[:-1] + (scales.shape[-1], array_shape[-1] // scales.shape[-1])
    )
    return (
        (blocked * scales.astype(jnp.float32)[..., None]).reshape(array_shape).astype(jnp.bfloat16)
    )


def route_tables(ids, counts, z_pos, tok_rows):
    count_float = counts.astype(jnp.float32)
    share = count_float / jnp.sum(count_float, axis=1, keepdims=True)
    experts = jnp.arange(X_SIZE, dtype=jnp.int32) * Z_SIZE + z_pos
    hit = ids[None] == experts[:, None, None]
    match = jnp.any(hit, axis=2)
    weight = jnp.sum(jnp.where(hit, share[None], 0.0), axis=2)
    ones = match.astype(jnp.bfloat16).reshape(X_SIZE * Z_SIZE, tok_rows)
    before = jnp.asarray(np.triu(np.ones((tok_rows, tok_rows)), 1), jnp.bfloat16)
    rank = jnp.dot(ones, before, preferred_element_type=jnp.float32).astype(jnp.int32)
    base = jnp.arange(Z_SIZE, dtype=jnp.int32)[None, :, None] * CAPACITY
    slot = (base + rank.reshape(X_SIZE, Z_SIZE, tok_rows)).reshape(X_SIZE, Z_SIZE * tok_rows)
    slot = jnp.where(match, slot, -1)
    lanes = jnp.arange(Z_SIZE * CAPACITY, dtype=jnp.int32)
    pick = slot[:, None, :] == lanes[None, :, None]
    slot_share = jnp.sum(jnp.where(pick, weight[:, None, :], 0.0), axis=2)
    pick = pick.reshape(X_SIZE * Z_SIZE * CAPACITY, Z_SIZE * tok_rows).astype(jnp.bfloat16)
    return (pick, slot_share.reshape(X_SIZE * Z_SIZE * CAPACITY))


def on_device(
    payload,
    block_scales,
    cotangent,
    expert_ids,
    route_counts,
    gate_up,
    down_weight,
    first_moment,
    second_moment,
):
    tok_rows, width = payload.shape
    replicas = lax.axis_size("rep")
    z_pos = lax.axis_index("exp") % Z_SIZE
    side = Z_SIZE * CAPACITY
    slot_count = X_SIZE * side
    activation = dequantize(payload, block_scales)
    routing = jnp.concatenate([expert_ids, route_counts], axis=1).astype(jnp.bfloat16)
    routing = jnp.pad(routing, ((0, 0), (0, 112)))
    act_all = lax.all_gather(
        jnp.concatenate([activation, routing], axis=1),
        "exp",
        axis=0,
        tiled=True,
        axis_index_groups=Z_GROUPS,
    )
    cot_all = lax.all_gather(cotangent, "exp", axis=0, tiled=True, axis_index_groups=Z_GROUPS)
    whole_gate_up = lax.all_gather(gate_up, "rep", axis=2, tiled=True)
    whole_down = lax.all_gather(down_weight, "rep", axis=2, tiled=True)
    top = expert_ids.shape[1]
    ids = act_all[:, width : width + top].astype(jnp.int32)
    counts = act_all[:, width + top : width + 2 * top].astype(jnp.int32)
    pick, slot_share = route_tables(ids, counts, z_pos, tok_rows)

    def to_experts(rows):
        return lax.all_to_all(
            rows.reshape(X_SIZE, side, width),
            "exp",
            split_axis=0,
            concat_axis=0,
            tiled=True,
            axis_index_groups=X_GROUPS,
        )

    act_rows = jnp.dot(pick, act_all[:, :width], preferred_element_type=jnp.float32)
    input_rows = to_experts(act_rows.astype(jnp.bfloat16)).reshape(slot_count, width)
    cot_rows = jnp.dot(pick, cot_all, preferred_element_type=jnp.float32)
    cot_rows = (slot_share[:, None] * cot_rows).astype(jnp.bfloat16)
    cotan_rows = to_experts(cot_rows).reshape(slot_count, width)
    pre_acts = jnp.einsum(
        "sd,tdf->tsf", input_rows, whole_gate_up[0], preferred_element_type=jnp.float32
    )
    hidden_grad = jnp.einsum(
        "sd,fd->sf", cotan_rows, whole_down[0], preferred_element_type=jnp.float32
    )
    silu_val, silu_slope = silu_parts(pre_acts[0])
    gate_grad = (hidden_grad * pre_acts[1] * silu_slope).astype(jnp.bfloat16)
    up_grad = (hidden_grad * silu_val).astype(jnp.bfloat16)
    row_grad = (
        jnp.einsum("sf,df->sd", gate_grad, whole_gate_up[0, 0], preferred_element_type=jnp.float32)
        + jnp.einsum("sf,df->sd", up_grad, whole_gate_up[0, 1], preferred_element_type=jnp.float32)
    ).astype(jnp.bfloat16)
    home = to_experts(row_grad).reshape(slot_count, width)
    partial = jnp.einsum("st,sd->td", pick, home, preferred_element_type=jnp.float32)
    d_activation = lax.psum_scatter(
        partial.astype(jnp.bfloat16),
        "exp",
        scatter_dimension=0,
        tiled=True,
        axis_index_groups=Z_GROUPS,
    )
    hidden_width = gate_grad.shape[1]
    both_grads = jnp.concatenate([gate_grad, up_grad], axis=1)
    term = jnp.einsum("sd,sf->df", input_rows, both_grads, preferred_element_type=jnp.float32)
    term = lax.optimization_barrier(term.astype(jnp.bfloat16))
    local_square = jnp.sum(jnp.square(term.astype(jnp.float32)))
    summed = lax.psum_scatter(term, "rep", scatter_dimension=0, tiled=True).astype(jnp.float32)
    shard_rows = width // replicas
    grad_shard = summed.reshape(shard_rows, 2, hidden_width).transpose(1, 0, 2)
    small_sum, big_sum = lax.psum((local_square, jnp.sum(jnp.square(grad_shard))), "rep")
    entry_count = 2.0 * width * hidden_width
    small_norm = small_sum / (replicas * entry_count)
    big_norm = big_sum / (replicas * replicas * entry_count)
    noise_gain = replicas * big_norm / (small_norm + 1e-06)
    new_first = 0.9 * first_moment + 0.1 * grad_shard[None]
    new_second = 0.95 * second_moment + 0.05 * jnp.square(grad_shard[None])
    weight_step = (noise_gain * new_first / (jnp.sqrt(new_second) + 1e-08)).astype(jnp.bfloat16)
    return (d_activation, new_first, new_second, weight_step)


def solution(mesh):
    tokens = P(("rep", "exp"), None)
    shards = P("exp", None, "rep", None)
    return jax.shard_map(
        on_device,
        mesh=mesh,
        in_specs=(tokens,) * 5 + (shards, P("exp", None, "rep"), shards, shards),
        out_specs=(tokens, shards, shards, shards),
        check_vma=False,
    )
```

profile of v0, /device:TPU:6, one launch (start us, length us, event | category | flops | bytes accessed | tf_op | source)
XLA Modules:
  0.0 364.9 jit_solution(17802854460447803655)
XLA Ops:
  7.2 0.8 copy.36
  8.0 0.8 copy.35
  8.8 0.8 copy.34
  9.7 1.0 fusion.22
  10.7 0.7 pad_maximum_fusion
  11.5 0.7 all-gather.7.cloned.1.call-update
  12.2 0.7 all-gather.11.cloned.1.call-update
  13.0 0.5 all-gather.9.cloned.1.call-update
  13.8 75.3 %all-gather.5.cloned.1.call-done = bf16[512,2176]{1,0:T(8,128)(2,1)} async-done(((bf16[32,2176]{1,0:T(8,128)(2,1)}), bf16[512,2176]{1,0:T(8,128)(2,1)}) %all-gather.5.cloned.1.call-update) | async-done | bytes 2228240 | tf_op jit(solution)/shard_map/all_gather | solution.py:68
  89.0 1.1 fusion.30
  91.0 3.5 convolution_convert_fusion.1
  94.5 4.8 %all-to-all-start.1 = ((bf16[4,80,2048]{2,1,0:T(8,128)(2,1)}), bf16[4,80,2048]{2,1,0:T(8,128)(2,1)S(1)}, u32[]{:S(2)}, u32[]{:S(2)}) async-start(bf16[4,80,2048]{2,1,0:T(8,128)(2,1)} %bitcast.4), calls=%async_computation.1 | async-start | bytes 2621440 | tf_op jit(solution)/shard_map/all_to_all | solution.py:84
  99.7 61.3 %all-gather.7.cloned.1.call-done = bf16[512,2048]{1,0:T(8,128)(2,1)} async-done(((bf16[32,2048]{1,0:T(8,128)(2,1)}), bf16[512,2048]{1,0:T(8,128)(2,1)}) %all-gather.7.cloned.1.call-update) | async-done | bytes 2097168 | tf_op jit(solution)/shard_map/all_gather | solution.py:75
  161.0 3.5 fusion.3
  164.5 4.8 %all-to-all-start = ((bf16[4,80,2048]{2,1,0:T(8,128)(2,1)}), bf16[4,80,2048]{2,1,0:T(8,128)(2,1)S(1)}, u32[]{:S(2)}, u32[]{:S(2)}) async-start(bf16[4,80,2048]{2,1,0:T(8,128)(2,1)} %bitcast.1), calls=%async_computation | async-start | bytes 2621440 | tf_op jit(solution)/shard_map/all_to_all | solution.py:84
  169.3 26.2 %all-gather.11.cloned.1.call-done = bf16[1,2,2048,384]{3,2,1,0:T(8,128)(2,1)} async-done(((bf16[1,2,256,384]{3,2,1,0:T(8,128)(2,1)}), bf16[1,2,2048,384]{3,2,1,0:T(8,128)(2,1)}) %all-gather.11.cloned.1.call-update) | async-done | bytes 3145744 | tf_op jit(solution)/shard_map/all_gather | solution.py:76
  195.5 4.0 %fusion.8 = f32[2,320,384]{2,1,0:T(8,128)} fusion(bf16[320,2048,1]{1,0,2:T(8,128)(2,1)S(1)} %bitcast.88, bf16[1,2,2048,384]{3,2,1,0:T(8,128)(2,1)} %all-gather.11.cloned.1.call-done), kind=kOutput, calls=%fused_computation.16 | convolution fusion | flops 1006632960 | bytes 5439488 | tf_op jit(solution)/shard_map/sd,tdf->tsf/dot_general | solution.py:98
  199.5 30.6 %all-gather.9.cloned.1.call-done = bf16[1,384,2048]{2,1,0:T(8,128)(2,1)} async-done(((bf16[1,384,256]{2,1,0:T(8,128)(2,1)}), bf16[1,384,2048]{2,1,0:T(8,128)(2,1)}) %all-gather.9.cloned.1.call-update) | async-done | bytes 1572880 | tf_op jit(solution)/shard_map/all_gather | solution.py:77
  230.1 2.6 multiply_convert_fusion
  232.7 0.7 copy-done.4
  233.4 3.5 convolution_convert_fusion
  237.0 1.8 copy-done.1
  238.8 0.9 fusion.5
  239.7 0.9 fusion.2
  240.6 20.8 %all_to_all.15 = bf16[4,80,2048]{2,1,0:T(8,128)(2,1)S(1)} all-to-all(bf16[4,80,2048]{2,1,0:T(8,128)(2,1)S(1)} %bitcast.85), channel_id=1, replica_groups={{0,16,32,48},{1,17,33,49},{2,18,34,50},{3,19,35,51},{4,20,36,52},{5,21,..., dimensions={0} | all-to-all | bytes 2621440 | tf_op jit(solution)/shard_map/all_to_all | solution.py:84
  261.5 2.7 bitcast_convert_fusion
  264.1 2.2 multiply_reduce_fusion
  266.4 15.5 %reduce-scatter.5.cloned.1.call-done = bf16[256,768]{1,0:T(8,128)(2,1)} async-done(((bf16[2048,768]{1,0:T(8,128)(2,1)}), bf16[256,768]{1,0:T(8,128)(2,1)}) %reduce-scatter.5.cloned.1.call-update) | async-done | bytes 393232 | tf_op jit(solution)/shard_map/reduce_scatter | solution.py:125
  281.8 1.8 convert_multiply_fusion.1
  283.6 13.5 %all-reduce.1 = (f32[]{:T(128)}, f32[]{:T(128)}) all-reduce(f32[]{:T(128)} %get-tuple-element.14, f32[]{:T(128)} %multiply_reduce_fusion), channel_id=1, replica_groups=mesh['rep'=8,'exp'=64] {'rep'}, use_global_device_ids=true, to_apply=%region_7.8 | all-reduce | flops 2 | bytes 16 | tf_op jit(solution)/shard_map/psum | solution.py:128
  298.5 1.4 divide_convert_fusion
  300.0 58.1 %reduce-scatter.3.cloned.1.call-done = bf16[32,2048]{1,0:T(8,128)(2,1)} async-done(((bf16[512,2048]{1,0:T(8,128)(2,1)}), bf16[32,2048]{1,0:T(8,128)(2,1)}) %reduce-scatter.3.cloned.1.call-update) | async-done | bytes 131088 | tf_op jit(solution)/shard_map/reduce_scatter | solution.py:113
  (48 shorter events, 2.1 us)
Async XLA Ops:
  7.2 83.3 %copy-start.6 = (bf16[32,32]{1,0:T(8,128)(2,1)S(1)}, bf16[32,32]{1,0:T(8,128)(2,1)}, u32[]{:S(2)}) copy-start(bf16[32,32]{1,0:T(8,128)(2,1)} %constant.52.clone) | copy-start | bytes 6148
  7.2 81.9 %all-gather.5.cloned.1.call-start = ((), (), s32[]{:S(2)}) async-start(), calls=%async_computation.5 | async-start | bytes 2367488 | tf_op jit(solution)/shard_map/all_gather | solution.py:68
  11.4 149.6 %all-gather.7.cloned.1.call-start = ((), (), s32[]{:S(2)}) async-start(), calls=%async_computation.6 | async-start | bytes 2228224 | tf_op jit(solution)/shard_map/all_gather | solution.py:75
  12.2 183.3 %all-gather.11.cloned.1.call-start = ((), (), s32[]{:S(2)}) async-start(), calls=%async_computation.8 | async-start | bytes 3538944 | tf_op jit(solution)/shard_map/all_gather | solution.py:76
  12.9 217.2 %all-gather.9.cloned.1.call-start = ((), (), s32[]{:S(2)}) async-start(), calls=%async_computation.7 | async-start | bytes 1769472 | tf_op jit(solution)/shard_map/all_gather | solution.py:77
  94.5 70.1 %all-to-all-start.1 = ((bf16[4,80,2048]{2,1,0:T(8,128)(2,1)}), bf16[4,80,2048]{2,1,0:T(8,128)(2,1)S(1)}, u32[]{:S(2)}, u32[]{:S(2)}) async-start(bf16[4,80,2048]{2,1,0:T(8,128)(2,1)} %bitcast.4), calls=%async_computation.1 | async-start | bytes 2621440 | tf_op jit(solution)/shard_map/all_to_all | solution.py:84
  164.5 65.6 %all-to-all-start = ((bf16[4,80,2048]{2,1,0:T(8,128)(2,1)}), bf16[4,80,2048]{2,1,0:T(8,128)(2,1)S(1)}, u32[]{:S(2)}, u32[]{:S(2)}) async-start(bf16[4,80,2048]{2,1,0:T(8,128)(2,1)} %bitcast.1), calls=%async_computation | async-start | bytes 2621440 | tf_op jit(solution)/shard_map/all_to_all | solution.py:84
  169.3 112.5 %reduce-scatter.5.cloned.1.call-start = ((), (), s32[]{:S(2)}) async-start(), calls=%async_computation.10 | async-start | bytes 3538944 | tf_op jit(solution)/shard_map/reduce_scatter | solution.py:125
  232.7 0.7 copy-start.4
  236.9 1.9 copy-start.1
  236.9 121.2 %reduce-scatter.3.cloned.1.call-start = ((), (), s32[]{:S(2)}) async-start(), calls=%async_computation.9 | async-start | bytes 2228224 | tf_op jit(solution)/shard_map/reduce_scatter | solution.py:113
  238.8 0.9 copy-start.5
  261.5 2.7 copy-start
  266.4 32.1 %copy-start.2 = (f32[1,2,256,384]{3,2,1,0:T(8,128)S(1)}, f32[1,2,256,384]{3,2,1,0:T(8,128)}, u32[]{:S(2)}) copy-start(f32[1,2,256,384]{3,2,1,0:T(8,128)} %param.18) | copy-start | bytes 2359300
  266.4 32.1 %copy-start.3 = (f32[1,2,256,384]{3,2,1,0:T(8,128)S(1)}, f32[1,2,256,384]{3,2,1,0:T(8,128)}, u32[]{:S(2)}) copy-start(f32[1,2,256,384]{3,2,1,0:T(8,128)} %param.17) | copy-start | bytes 2359300
Sparse Core Ops, SparseCore 0:
  11.6 77.4 all-gather.4
  91.1 69.8 all-gather.6
  163.2 32.2 all-gather.10
  197.4 32.5 all-gather.8
  237.0 44.7 reduce-scatter.4
  285.1 72.9 reduce-scatter.2
where the time goes:
time: 366 us; the launch traced here: 365 us
  waiting for transfers between devices  269 us (73%)
  blocking collectives  34.4 us (9%)
  matrix products  21.7 us (6%)
  between operations  15.6 us (4%)
  starting transfers between devices  9.77 us (3%)
  other arithmetic  7.83 us (2%)
  local copies, waits for them, and re-layouts  6.8 us (2%)
    all_gather x1, waiting for transfers between devices, on_device(): lax.all_gather(jnp.concatenate([activation, routing], axis=1), 'exp', axi...  75.3 us
    all_gather x1, waiting for transfers between devices, on_device(): lax.all_gather(cotangent, 'exp', axis=0, tiled=True, axis_index_groups=Z_...  61.3 us
    reduce_scatter x1, waiting for transfers between devices, on_device(): lax.psum_scatter(partial.astype(jnp.bfloat16), 'exp', scatter_dimension=0...  58.1 us
    all_gather x1, waiting for transfers between devices, on_device(): whole_down = lax.all_gather(down_weight, 'rep', axis=2, tiled=True)  30.6 us
    all_gather x1, waiting for transfers between devices, on_device(): whole_gate_up = lax.all_gather(gate_up, 'rep', axis=2, tiled=True)  26.2 us
    all_to_all x1, blocking collectives, to_experts(): lax.all_to_all(rows.reshape(X_SIZE, side, width), 'exp', split_axis=0, co...  20.8 us
    reduce_scatter x1, waiting for transfers between devices, on_device(): lax.psum_scatter(term, 'rep', scatter_dimension=0, tiled=True)  15.5 us
    psum x1, blocking collectives, on_device(): lax.psum((local_square, jnp.sum(jnp.square(grad_shard))), 'rep')  13.5 us
  transfers between devices with their start and end apart: 8, of which 6 were waited for; matrix products, arithmetic and copies ran while one was open for 6% of the time, Pallas kernels for 0%

commit v1 on v0

--- a/solution.py
+++ b/solution.py
@@ -74,7 +74,19 @@
     )
     cot_all = lax.all_gather(cotangent, "exp", axis=0, tiled=True, axis_index_groups=Z_GROUPS)
     whole_gate_up = lax.all_gather(gate_up, "rep", axis=2, tiled=True)
-    whole_down = lax.all_gather(down_weight, "rep", axis=2, tiled=True)
+    axis_len = lax.axis_size("rep")
+    column = [(dd, (dd + 1) % axis_len) for dd in range(axis_len)]
+    crops = [(dd, (dd - 1) % axis_len) for dd in range(axis_len)]
+    q_next, g_now = ([down_weight], [down_weight])
+    for _ in range(axis_len // 2):
+        q_next.append(lax.ppermute(q_next[-1], axis_name="rep", perm=column))
+    for _ in range((axis_len - 1) // 2):
+        g_now.append(lax.ppermute(g_now[-1], axis_name="rep", perm=crops))
+    whole_down = jnp.roll(
+        jnp.concatenate([*q_next[::-1], *g_now[1:]], 2),
+        (lax.axis_index("rep") - axis_len // 2) * down_weight.shape[2],
+        2,
+    )
     top = expert_ids.shape[1]
     ids = act_all[:, width : width + top].astype(jnp.int32)
     counts = act_all[:, width + top : width + 2 * top].astype(jnp.int32)

time: 366 us -> 334 us (0.913)
  waiting for transfers between devices: 269 us -> 214 us
  local copies, waits for them, and re-layouts: 6.8 us -> 19.3 us
  starting transfers between devices: 9.77 us -> 18.6 us
    all_gather x1, waiting for transfers between devices: 75.3 us -> 43.5 us  [on_device(): lax.all_gather(jnp.concatenate([activation, routing], axis=1), 'exp', axi...]
    all_gather x1 -> x0, waiting for transfers between devices: 30.6 us -> none  [on_device(): whole_down = lax.all_gather(down_weight, 'rep', axis=2, tiled=True)]
    ppermute x0 -> x7, waiting for transfers between devices: none -> 16.2 us  [the longest x4 16.1 us: on_device(): q_next.append(lax.ppermute(q_next[-1], axis_name='rep', perm=column))]
    unnamed x18 -> x33, local copies, waits for them, and re-layouts: 4.26 us -> 15.1 us
    ppermute x0 -> x7, starting transfers between devices: none -> 8.99 us  [the longest x3 8.96 us: on_device(): g_now.append(lax.ppermute(g_now[-1], axis_name='rep', perm=crops))]
    all_gather x1, waiting for transfers between devices: 26.2 us -> 21.6 us  [on_device(): whole_gate_up = lax.all_gather(gate_up, 'rep', axis=2, tiled=True)]
  transfers between devices with their start and end apart: 8 -> 14, of which waited for: 6 -> 10; matrix products, arithmetic and copies ran while one was open for 6% -> 11% of each run, Pallas kernels for 0% -> 0%
where the time goes in v1:
time: 334 us; the launch traced here: 333 us
  waiting for transfers between devices  214 us (64%)
  blocking collectives  34.3 us (10%)
  matrix products  21.8 us (7%)
  local copies, waits for them, and re-layouts  19.3 us (6%)
  starting transfers between devices  18.6 us (6%)
  between operations  15.3 us (5%)
  other arithmetic  9.21 us (3%)
    all_gather x1, waiting for transfers between devices, on_device(): lax.all_gather(cotangent, 'exp', axis=0, tiled=True, axis_index_groups=Z_...  60.6 us
    reduce_scatter x1, waiting for transfers between devices, on_device(): lax.psum_scatter(partial.astype(jnp.bfloat16), 'exp', scatter_dimension=0...  56.4 us
    all_gather x1, waiting for transfers between devices, on_device(): lax.all_gather(jnp.concatenate([activation, routing], axis=1), 'exp', axi...  43.5 us
    all_gather x1, waiting for transfers between devices, on_device(): whole_gate_up = lax.all_gather(gate_up, 'rep', axis=2, tiled=True)  21.6 us
    all_to_all x1, blocking collectives, to_experts(): lax.all_to_all(rows.reshape(X_SIZE, side, width), 'exp', split_axis=0, co...  20.8 us
    ppermute x4, waiting for transfers between devices, on_device(): q_next.append(lax.ppermute(q_next[-1], axis_name='rep', perm=column))  16.1 us
    unnamed x33, local copies, waits for them, and re-layouts  15.1 us
    reduce_scatter x1, waiting for transfers between devices, on_device(): lax.psum_scatter(term, 'rep', scatter_dimension=0, tiled=True)  14.6 us
  transfers between devices with their start and end apart: 14, of which 10 were waited for; matrix products, arithmetic and copies ran while one was open for 11% of the time, Pallas kernels for 0%

profile of v1, /device:TPU:6, one launch (start us, length us, event | category | flops | bytes accessed | tf_op | source)
XLA Modules:
  0.0 332.8 jit_solution(4770232278290792577)
XLA Ops:
  7.2 0.8 copy.34
  9.8 1.0 fusion.23
  13.0 6.5 %collective-permute-done = bf16[1,384,256]{2,1,0:T(8,128)(2,1)S(1)} collective-permute-done((bf16[1,384,256]{2,1,0:T(8,128)(2,1)}, bf16[1,384,256]{2,1,0:T(8,128)(2,1)S(1)}, u32[]{:S(2)}, u32[]{:S(2)}) %collective-permute-start) | collective-permute-done | bytes 196640 | tf_op jit(solution)/shard_map/ppermute | solution.py:82
  19.5 3.0 collective-permute-start.4
  22.5 3.3 %collective-permute-done.1 = bf16[1,384,256]{2,1,0:T(8,128)(2,1)S(1)} collective-permute-done((bf16[1,384,256]{2,1,0:T(8,128)(2,1)S(1)}, bf16[1,384,256]{2,1,0:T(8,128)(2,1)S(1)}, u32[]{:S(2)}, u32[]{:S(2)}) %collective-permute-start.1) | collective-permute-done | bytes 196640 | tf_op jit(solution)/shard_map/ppermute | solution.py:82
  26.0 3.0 collective-permute-start.5
  29.0 3.1 collective-permute-done.2
  32.3 3.0 collective-permute-start.6
  35.3 3.1 collective-permute-done.3
  45.6 43.5 %all-gather.4.cloned.1.call-done = bf16[512,2176]{1,0:T(8,128)(2,1)} async-done(((bf16[32,2176]{1,0:T(8,128)(2,1)}), bf16[512,2176]{1,0:T(8,128)(2,1)}) %all-gather.4.cloned.1.call-update) | async-done | bytes 2228240 | tf_op jit(solution)/shard_map/all_gather | solution.py:68
  89.1 1.1 fusion.32
  91.0 3.5 %convolution_convert_fusion.1 = bf16[320,2048]{1,0:T(8,128)(2,1)} fusion(pred[320,512]{1,0:T(32,128)(4,1)S(1)} %bitcast_compare_fusion, bf16[512,2176]{1,0:T(8,128)(2,1)} %all-gather.4.cloned.1.call-done), kind=kOutput, calls=%fused_computation.9 | convolution fusion | flops 671744000 | bytes 3571712 | tf_op jit(solution)/shard_map/dot_general | solution.py:105
  94.5 4.7 %all-to-all-start.1 = ((bf16[4,80,2048]{2,1,0:T(8,128)(2,1)}), bf16[4,80,2048]{2,1,0:T(8,128)(2,1)S(1)}, u32[]{:S(2)}, u32[]{:S(2)}) async-start(bf16[4,80,2048]{2,1,0:T(8,128)(2,1)} %bitcast.4), calls=%async_computation.1 | async-start | bytes 2621440 | tf_op jit(solution)/shard_map/all_to_all | solution.py:96
  100.4 60.6 %all-gather.6.cloned.1.call-done = bf16[512,2048]{1,0:T(8,128)(2,1)} async-done(((bf16[32,2048]{1,0:T(8,128)(2,1)}), bf16[512,2048]{1,0:T(8,128)(2,1)}) %all-gather.6.cloned.1.call-update) | async-done | bytes 2097168 | tf_op jit(solution)/shard_map/all_gather | solution.py:75
  161.0 3.5 %fusion.3 = bf16[320,2048]{1,0:T(8,128)(2,1)} fusion(pred[320,512]{1,0:T(32,128)(4,1)S(1)} %bitcast_compare_fusion, bf16[512,2048]{1,0:T(8,128)(2,1)} %all-gather.6.cloned.1.call-done, f32[320]{0:T(512)S(1)} %mul.110), kind=kOutput, calls=%fused_computation.8 | convolution fusion | flops 672399360 | bytes 3572992 | tf_op jit(solution)/shard_map/dot_general | solution.py:107
  164.5 4.8 %all-to-all-start = ((bf16[4,80,2048]{2,1,0:T(8,128)(2,1)}), bf16[4,80,2048]{2,1,0:T(8,128)(2,1)S(1)}, u32[]{:S(2)}, u32[]{:S(2)}) async-start(bf16[4,80,2048]{2,1,0:T(8,128)(2,1)} %bitcast.1), calls=%async_computation | async-start | bytes 2621440 | tf_op jit(solution)/shard_map/all_to_all | solution.py:96
  172.2 1.6 constant_dynamic-update-slice_fusion
  173.9 21.6 %all-gather.8.cloned.1.call-done = bf16[1,2,2048,384]{3,2,1,0:T(8,128)(2,1)} async-done(((bf16[1,2,256,384]{3,2,1,0:T(8,128)(2,1)}), bf16[1,2,2048,384]{3,2,1,0:T(8,128)(2,1)}) %all-gather.8.cloned.1.call-update) | async-done | bytes 3145744 | tf_op jit(solution)/shard_map/all_gather | solution.py:76
  195.4 4.1 %fusion.9 = f32[2,320,384]{2,1,0:T(8,128)} fusion(bf16[320,2048,1]{1,0,2:T(8,128)(2,1)S(1)} %bitcast.88, bf16[1,2,2048,384]{3,2,1,0:T(8,128)(2,1)} %all-gather.8.cloned.1.call-done), kind=kOutput, calls=%fused_computation.17 | convolution fusion | flops 1006632960 | bytes 5439488 | tf_op jit(solution)/shard_map/sd,tdf->tsf/dot_general | solution.py:110
  199.6 2.6 multiply_convert_fusion
  202.8 3.5 %convolution_convert_fusion = bf16[2048,768]{1,0:T(8,128)(2,1)} fusion(bf16[320,2048]{1,0:T(8,128)(2,1)S(1)} %bitcast.89, bf16[320,384]{1,0:T(8,128)(2,1)S(1)} %get-tuple-element.11, bf16[320,384]{1,0:T(8,128)(2,1)S(1)} %get-tuple-element.12), kind=kOutput, calls=%fused_computation.2 | convolution fusion | flops 1009188864 | bytes 4947968 | tf_op jit(solution)/shard_map/sd,sf->df/dot_general | solution.py:134
  206.4 1.8 copy-done.1
  208.2 0.9 fusion.5
  209.2 0.9 fusion.2
  210.1 20.8 %all_to_all.15 = bf16[4,80,2048]{2,1,0:T(8,128)(2,1)S(1)} all-to-all(bf16[4,80,2048]{2,1,0:T(8,128)(2,1)S(1)} %bitcast.85), channel_id=1, replica_groups={{0,16,32,48},{1,17,33,49},{2,18,34,50},{3,19,35,51},{4,20,36,52},{5,21,..., dimensions={0} | all-to-all | bytes 2621440 | tf_op jit(solution)/shard_map/all_to_all | solution.py:96
  230.9 2.6 bitcast_convert_fusion
  233.6 2.2 multiply_reduce_fusion
  235.8 14.6 %reduce-scatter.5.cloned.1.call-done = bf16[256,768]{1,0:T(8,128)(2,1)} async-done(((bf16[2048,768]{1,0:T(8,128)(2,1)}), bf16[256,768]{1,0:T(8,128)(2,1)}) %reduce-scatter.5.cloned.1.call-update) | async-done | bytes 393232 | tf_op jit(solution)/shard_map/reduce_scatter | solution.py:137
  250.4 1.8 convert_multiply_fusion.1
  252.2 13.5 %all-reduce.1 = (f32[]{:T(128)}, f32[]{:T(128)}) all-reduce(f32[]{:T(128)} %get-tuple-element.14, f32[]{:T(128)} %multiply_reduce_fusion), channel_id=1, replica_groups=mesh['rep'=8,'exp'=64] {'rep'}, use_global_device_ids=true, to_apply=%region_7.8 | all-reduce | flops 2 | bytes 16 | tf_op jit(solution)/shard_map/psum | solution.py:140
  267.0 2.8 divide_convert_fusion
  269.8 56.4 %reduce-scatter.3.cloned.1.call-done = bf16[32,2048]{1,0:T(8,128)(2,1)} async-done(((bf16[512,2048]{1,0:T(8,128)(2,1)}), bf16[32,2048]{1,0:T(8,128)(2,1)}) %reduce-scatter.3.cloned.1.call-update) | async-done | bytes 131088 | tf_op jit(solution)/shard_map/reduce_scatter | solution.py:125
  (75 shorter events, 17.2 us)
Async XLA Ops:
  7.2 34.2 %copy-start.2 = (bf16[1,384,256]{2,1,0:T(8,128)(2,1)S(1)}, bf16[1,384,256]{2,1,0:T(8,128)(2,1)}, u32[]{:S(2)}) copy-start(bf16[1,384,256]{2,1,0:T(8,128)(2,1)} %param.16) | copy-start | bytes 589828
  7.2 81.9 %all-gather.4.cloned.1.call-start = ((), (), s32[]{:S(2)}) async-start(), calls=%async_computation.5 | async-start | bytes 2367488 | tf_op jit(solution)/shard_map/all_gather | solution.py:68
  9.8 80.7 %copy-start.6 = (bf16[32,32]{1,0:T(8,128)(2,1)S(1)}, bf16[32,32]{1,0:T(8,128)(2,1)}, u32[]{:S(2)}) copy-start(bf16[32,32]{1,0:T(8,128)(2,1)} %constant.83.clone) | copy-start | bytes 6148
  11.5 149.5 %all-gather.6.cloned.1.call-start = ((), (), s32[]{:S(2)}) async-start(), calls=%async_computation.6 | async-start | bytes 2228224 | tf_op jit(solution)/shard_map/all_gather | solution.py:75
  12.2 183.2 %all-gather.8.cloned.1.call-start = ((), (), s32[]{:S(2)}) async-start(), calls=%async_computation.7 | async-start | bytes 3538944 | tf_op jit(solution)/shard_map/all_gather | solution.py:76
  13.0 6.5 %collective-permute-start = (bf16[1,384,256]{2,1,0:T(8,128)(2,1)}, bf16[1,384,256]{2,1,0:T(8,128)(2,1)S(1)}, u32[]{:S(2)}, u32[]{:S(2)}) collective-permute-start(bf16[1,384,256]{2,1,0:T(8,128)(2,1)} %param.16), channel_id=1, source_target_pairs={{0,64},{64,128},{128,192},{192,256},{256,320},{320,384},{384,448},... | collective-permute-start | bytes 589832 | tf_op jit(solution)/shard_map/ppermute | solution.py:82
  19.5 6.3 %collective-permute-start.1 = (bf16[1,384,256]{2,1,0:T(8,128)(2,1)S(1)}, bf16[1,384,256]{2,1,0:T(8,128)(2,1)S(1)}, u32[]{:S(2)}, u32[]{:S(2)}) collective-permute-start(bf16[1,384,256]{2,1,0:T(8,128)(2,1)S(1)} %collective-permute-done), channel_id=1, source_target_pairs={{0,64},{64,128},{128,192},{192,256},{256,320},{320,384},{384,448},... | collective-permute-start | bytes 589832 | tf_op jit(solution)/shard_map/ppermute | solution.py:82
  19.5 6.5 %collective-permute-start.4 = (bf16[1,384,256]{2,1,0:T(8,128)(2,1)}, bf16[1,384,256]{2,1,0:T(8,128)(2,1)S(1)}, u32[]{:S(2)}, u32[]{:S(2)}) collective-permute-start(bf16[1,384,256]{2,1,0:T(8,128)(2,1)} %param.16), channel_id=1, source_target_pairs={{0,448},{64,0},{128,64},{192,128},{256,192},{320,256},{384,320},{4... | collective-permute-start | bytes 589832 | tf_op jit(solution)/shard_map/ppermute | solution.py:84
  25.8 6.3 %collective-permute-start.2 = (bf16[1,384,256]{2,1,0:T(8,128)(2,1)S(1)}, bf16[1,384,256]{2,1,0:T(8,128)(2,1)S(1)}, u32[]{:S(2)}, u32[]{:S(2)}) collective-permute-start(bf16[1,384,256]{2,1,0:T(8,128)(2,1)S(1)} %collective-permute-done.1), channel_id=1, source_target_pairs={{0,64},{64,128},{128,192},{192,256},{256,320},{320,384},{384,448},... | collective-permute-start | bytes 589832 | tf_op jit(solution)/shard_map/ppermute | solution.py:82
  26.0 6.3 %collective-permute-start.5 = (bf16[1,384,256]{2,1,0:T(8,128)(2,1)S(1)}, bf16[1,384,256]{2,1,0:T(8,128)(2,1)S(1)}, u32[]{:S(2)}, u32[]{:S(2)}) collective-permute-start(bf16[1,384,256]{2,1,0:T(8,128)(2,1)S(1)} %collective-permute-done.4), channel_id=1, source_target_pairs={{0,448},{64,0},{128,64},{192,128},{256,192},{320,256},{384,320},{4... | collective-permute-start | bytes 589832 | tf_op jit(solution)/shard_map/ppermute | solution.py:84
  32.1 6.3 %collective-permute-start.3 = (bf16[1,384,256]{2,1,0:T(8,128)(2,1)S(1)}, bf16[1,384,256]{2,1,0:T(8,128)(2,1)S(1)}, u32[]{:S(2)}, u32[]{:S(2)}) collective-permute-start(bf16[1,384,256]{2,1,0:T(8,128)(2,1)S(1)} %collective-permute-done.2), channel_id=1, source_target_pairs={{0,64},{64,128},{128,192},{192,256},{256,320},{320,384},{384,448},... | collective-permute-start | bytes 589832 | tf_op jit(solution)/shard_map/ppermute | solution.py:82
  32.3 11.2 %collective-permute-start.6 = (bf16[1,384,256]{2,1,0:T(8,128)(2,1)S(1)}, bf16[1,384,256]{2,1,0:T(8,128)(2,1)S(1)}, u32[]{:S(2)}, u32[]{:S(2)}) collective-permute-start(bf16[1,384,256]{2,1,0:T(8,128)(2,1)S(1)} %collective-permute-done.5), channel_id=1, source_target_pairs={{0,448},{64,0},{128,64},{192,128},{256,192},{320,256},{384,320},{4... | collective-permute-start | bytes 589832 | tf_op jit(solution)/shard_map/ppermute | solution.py:84
  43.5 121.0 %copy-start.3 = (bf16[1,384,256]{2,1,0:T(8,128)(2,1)}, bf16[1,384,256]{2,1,0:T(8,128)(2,1)S(1)}, u32[]{:S(2)}) copy-start(bf16[1,384,256]{2,1,0:T(8,128)(2,1)S(1)} %collective-permute-done.6) | copy-start | bytes 589828
  94.5 70.0 %all-to-all-start.1 = ((bf16[4,80,2048]{2,1,0:T(8,128)(2,1)}), bf16[4,80,2048]{2,1,0:T(8,128)(2,1)S(1)}, u32[]{:S(2)}, u32[]{:S(2)}) async-start(bf16[4,80,2048]{2,1,0:T(8,128)(2,1)} %bitcast.4), calls=%async_computation.1 | async-start | bytes 2621440 | tf_op jit(solution)/shard_map/all_to_all | solution.py:96
  164.5 35.0 %all-to-all-start = ((bf16[4,80,2048]{2,1,0:T(8,128)(2,1)}), bf16[4,80,2048]{2,1,0:T(8,128)(2,1)S(1)}, u32[]{:S(2)}, u32[]{:S(2)}) async-start(bf16[4,80,2048]{2,1,0:T(8,128)(2,1)} %bitcast.1), calls=%async_computation | async-start | bytes 2621440 | tf_op jit(solution)/shard_map/all_to_all | solution.py:96
  169.3 81.1 %reduce-scatter.5.cloned.1.call-start = ((), (), s32[]{:S(2)}) async-start(), calls=%async_computation.9 | async-start | bytes 3538944 | tf_op jit(solution)/shard_map/reduce_scatter | solution.py:137
  202.1 0.7 copy-start.4
  206.3 1.9 copy-start.1
  206.4 119.9 %reduce-scatter.3.cloned.1.call-start = ((), (), s32[]{:S(2)}) async-start(), calls=%async_computation.8 | async-start | bytes 2228224 | tf_op jit(solution)/shard_map/reduce_scatter | solution.py:125
  208.2 0.9 copy-start.5
  230.9 2.7 copy-start
Sparse Core Ops, SparseCore 0:
  11.6 77.4 all-gather.3
  91.2 69.7 all-gather.5
  163.1 32.2 all-gather.7
  206.5 43.8 reduce-scatter.4
  253.6 72.5 reduce-scatter.2
